TPU v7x, 32 devices: a whole 2x2x4 slice. The times are simulated.
32 devices in a mesh: dp: 8 (over y, x, core), mp: 4 (over z).
Axes of the slice: x: 2, y: 2, z: 4, core: 2. Of those that a mesh axis runs over, the one named last changes fastest.
Arguments:
- tokens: bfloat16 [1536, 8192], P(None, 'dp'), may hold values from -6 to 6
- gate_weight: bfloat16 [8192, 15360], P('dp', 'mp'), may hold values from -0.0625 to 0.0625
- up_weight: bfloat16 [8192, 15360], P('dp', 'mp'), may hold values from -0.0625 to 0.0625
- down_weight: bfloat16 [15360, 8192], P('mp', 'dp'), may hold values from -0.046875 to 0.046875
Outputs:
- mixed: bfloat16 [1536, 8192], P('mp', 'dp')
All inputs are finite; a program needn't handle non-finite values.
Results may differ from a plain program's by a relative error of at most 0.0049.
Values may be sent and summed in bfloat16 or wider, within the bound.
No kernel may reach another device: no remote copies, remote signals or barrier semaphores. Data moves between devices by JAX's collectives and lax.ppermute only.
A program may use at most 192 MiB of HBM per device.

v0:
```python
import jax
import jax.numpy as jnp
from jax import lax
from jax.sharding import PartitionSpec as P


def body(tokens, gate_weight, up_weight, down_weight):
    group = gate_weight.shape[1]
    both_weights = jnp.concatenate((gate_weight, up_weight), axis=1)
    summed = lax.psum_scatter(
        jnp.dot(tokens, both_weights, preferred_element_type=jnp.float32),
        "dp",
        scatter_dimension=0,
        tiled=True,
    )
    hidden = (jax.nn.silu(summed[:, :group]) * summed[:, group:]).astype(jnp.bfloat16)
    partial_out = jnp.dot(
        lax.all_gather(hidden, "dp", axis=0, tiled=True),
        down_weight,
        preferred_element_type=jnp.float32,
    )
    mixed = lax.psum_scatter(partial_out, "mp", scatter_dimension=0, tiled=True)
    return mixed.astype(jnp.bfloat16)


def solution(mesh):
    in_specs = (P(None, "dp"), P("dp", "mp"), P("dp", "mp"), P("mp", "dp"))
    out_specs = P("mp", "dp")
    return jax.shard_map(body, mesh=mesh, in_specs=in_specs, out_specs=out_specs, check_vma=False)
```

profile of v0, /device:TPU:0, one launch (start us, length us, event | category | flops | bytes accessed | tf_op | source)
XLA Modules:
  0.0 585.4 jit_solution(2839760742585564814)
XLA Ops:
  6.5 0.0 copy-start
  6.5 0.0 reduce-scatter.7.cloned.1.call-start
  6.5 1.9 copy-done
  8.4 32.1 %convolution_bitcast_fusion = f32[1536,7680]{0,1:T(8,128)} fusion(bf16[1536,1024]{1,0:T(8,128)(2,1)S(1)} %copy-done, bf16[1024,3840]{1,0:T(8,128)(2,1)} %param.6, bf16[1024,3840]{1,0:T(8,128)(2,1)} %param.5), kind=kOutput, calls=%fused_computation | convolution fusion | flops 24190648320 | bytes 66060288 | tf_op jit(solution)/shard_map/dot_general | solution.py:11
  40.5 45.9 %copy.6 = f32[1536,7680]{1,0:T(8,128)} copy(f32[1536,7680]{0,1:T(8,128)} %convolution_bitcast_fusion) | data formatting | bytes 94371840
  86.4 0.0 reduce-scatter.7.cloned.1.call-update
  86.4 0.0 all-gather.2.cloned.1.call-start
  86.4 272.3 %reduce-scatter.7.cloned.1.call-done = f32[192,7680]{1,0:T(8,128)} async-done(((f32[1536,7680]{1,0:T(8,128)}), f32[192,7680]{1,0:T(8,128)}) %reduce-scatter.7.cloned.1.call-update) | async-done | bytes 5898256
  358.7 4.7 fusion.4
  363.4 5.0 copy.8
  368.4 3.1 copy.9
  371.5 4.4 multiply_convert_fusion
  375.9 2.2 copy.5
  378.1 0.0 all-gather.2.cloned.1.call-update
  378.1 0.2 reduce-scatter.5.cloned.1.call-start
  378.3 68.6 %all-gather.2.cloned.1.call-done = bf16[1536,3840]{1,0:T(8,128)(2,1)} async-done(((bf16[192,3840]{1,0:T(8,128)(2,1)}), bf16[1536,3840]{1,0:T(8,128)(2,1)}) %all-gather.2.cloned.1.call-update) | async-done | bytes 11796496 | tf_op jit(solution)/shard_map/all_gather | solution.py:18
  446.9 0.0 copy-start.1
  446.9 18.6 %fusion.5 = f32[1536,1024]{1,0:T(8,128)} fusion(bf16[1536,3840]{1,0:T(8,128)(2,1)} %all-gather.2.cloned.1.call-done, bf16[3840,1024]{1,0:T(8,128)(2,1)} %param.7), kind=kOutput, calls=%fused_computation.7 | convolution fusion | flops 12079595520 | bytes 25952256 | tf_op jit(solution)/shard_map/dot_general | solution.py:17
  465.5 0.0 reduce-scatter.5.cloned.1.call-update
  465.5 110.9 %reduce-scatter.5.cloned.1.call-done = f32[384,1024]{1,0:T(8,128)} async-done(((f32[1536,1024]{1,0:T(8,128)}), f32[384,1024]{1,0:T(8,128)}) %reduce-scatter.5.cloned.1.call-update) | async-done | bytes 1572880 | tf_op jit(solution)/shard_map/reduce_scatter | solution.py:22
  576.5 2.4 convert_element_type.7
  578.9 0.0 copy-done.1
Async XLA Ops:
  6.5 1.9 copy-start
  6.5 352.1 %reduce-scatter.7.cloned.1.call-start = ((), (), s32[]{:S(2)}) async-start(), calls=%async_computation.4 | async-start | bytes 53084160
  86.4 360.6 %all-gather.2.cloned.1.call-start = ((), (), s32[]{:S(2)}) async-start(), calls=%async_computation.2 | async-start | bytes 13271040 | tf_op jit(solution)/shard_map/all_gather | solution.py:18
  378.1 198.4 %reduce-scatter.5.cloned.1.call-start = ((), (), s32[]{:S(2)}) async-start(), calls=%async_computation.3 | async-start | bytes 7864320 | tf_op jit(solution)/shard_map/reduce_scatter | solution.py:22
  446.9 131.9 %copy-start.1 = (bf16[1536,1024]{1,0:T(8,128)(2,1)S(1)}, bf16[1536,1024]{1,0:T(8,128)(2,1)}, u32[]{:S(2)}) copy-start(bf16[1536,1024]{1,0:T(8,128)(2,1)} %param.4) | copy-start | bytes 9437188
Sparse Core Ops, SparseCore 0:
  86.5 272.1 reduce-scatter.6
  378.2 68.6 all-gather.1
  465.7 110.7 reduce-scatter.4
where the time goes:
time: 586 us; the launch traced here: 585 us
  waiting for transfers between devices  452 us (77%)
  local copies, waits for them, and re-layouts  62.7 us (11%)
  matrix products  50.6 us (9%)
  between operations  13.1 us (2%)
  other arithmetic  6.84 us (1%)
    unnamed x4, waiting for transfers between devices  272 us
    reduce_scatter x1, waiting for transfers between devices, body(): mixed = lax.psum_scatter(partial_out, 'mp', scatter_dimension=0, tiled=True)  111 us
    all_gather x1, waiting for transfers between devices, body(): lax.all_gather(hidden, 'dp', axis=0, tiled=True)  68.6 us
    unnamed x7, local copies, waits for them, and re-layouts  55.8 us
    dot_general x1, matrix products, body(): jnp.dot(tokens, both_weights, preferred_element_type=jnp.float32)  32.1 us
    dot_general x1, matrix products, body(): jnp.dot(lax.all_gather(hidden, 'dp', axis=0, tiled=True), down_weight, pr...  18.6 us
  transfers between devices with their start and end apart: 3, of which 3 were waited for; matrix products, arithmetic and copies ran while one was open for 0% of the time, Pallas kernels for 0%

commit v1 on v0

v1 whole, which is shorter than its diff:
```python
import jax
import jax.numpy as jnp
from jax import lax
from jax.experimental import pallas as pl
from jax.experimental.pallas import tpu as pltpu
from jax.sharding import PartitionSpec as P


F32, BF16 = jnp.float32, jnp.bfloat16
MIB = 1 << 20
ANY = pl.BlockSpec(memory_space=pl.ANY)
VMEM = pl.BlockSpec(memory_space=pltpu.VMEM)
SMEM = pl.BlockSpec(memory_space=pltpu.SMEM)
LIMIT = 16
ALONE = 17
ROWS = 8


def tile_of(extent, most):
    return max(t for t in range(128, min(extent, most) + 1, 128) if extent % t == 0)


def gather_rows(where, tokens, lists, sizes, limit=8):
    depth = tokens.shape[1]
    block = tokens.shape[0] // 4
    count = sum(map(len, lists))

    def kernel(where_ref, tokens_ref, *refs):
        outs, sems = refs[:-1], refs[-1]
        copies = []
        for out, places, s in zip(outs, lists, sizes):
            for n, (place, at) in enumerate(places):
                first = pl.multiple_of((where_ref[2] ^ place) * block + at, 16)
                copies.append(
                    pltpu.make_async_copy(
                        tokens_ref.at[pl.ds(first, s)], out.at[pl.ds(n * s, s)], sems.at[len(copies)]
                    )
                )
        for copy in copies:
            copy.start()
        for copy in copies:
            copy.wait()

    return pl.pallas_call(
        kernel,
        out_shape=[jax.ShapeDtypeStruct((len(p) * s, depth), BF16) for p, s in zip(lists, sizes)],
        in_specs=[SMEM, ANY],
        out_specs=[VMEM] * len(lists),
        scratch_shapes=[pltpu.SemaphoreType.DMA((count,))],
        cost_estimate=pl.CostEstimate(flops=0, bytes_accessed=4 * tokens.size, transcendentals=0),
        compiler_params=pltpu.CompilerParams(vmem_limit_bytes=limit * MIB),
        name="gather_rows",
    )(where, tokens)


def halves(where, weight, cuts, limit):
    depth, half = weight.shape[0], weight.shape[1] // 2
    spans = [(0, 0, half)]
    for size in cuts:
        spans.append((1, sum(size for side, _, size in spans if side), size))

    def kernel(where_ref, w, *refs):
        sems = refs[-1]
        copies = [
            pltpu.make_async_copy(
                w.at[:, pl.ds(pl.multiple_of((side ^ where_ref[0]) * half + at, 128), size)], out, sems.at[n]
            )
            for n, (out, (side, at, size)) in enumerate(zip(refs[:-1], spans))
        ]
        for copy in copies:
            copy.start()
        for copy in copies:
            copy.wait()

    return pl.pallas_call(
        kernel,
        out_shape=[jax.ShapeDtypeStruct((depth, size), BF16) for _, _, size in spans],
        in_specs=[SMEM, ANY],
        out_specs=[VMEM] * len(spans),
        scratch_shapes=[pltpu.SemaphoreType.DMA((len(spans),))],
        cost_estimate=pl.CostEstimate(flops=0, bytes_accessed=8 * depth * half, transcendentals=0),
        compiler_params=pltpu.CompilerParams(vmem_limit_bytes=limit * MIB),
        name="halves",
    )(where, weight)


def bring(value):
    def kernel(source, out, sem):
        copy = pltpu.make_async_copy(source, out, sem)
        copy.start()
        copy.wait()

    return pl.pallas_call(
        kernel,
        out_shape=jax.ShapeDtypeStruct(value.shape, value.dtype),
        in_specs=[ANY],
        out_specs=VMEM,
        scratch_shapes=[pltpu.SemaphoreType.DMA],
        cost_estimate=pl.CostEstimate(flops=0, bytes_accessed=4 * value.size, transcendentals=0),
        compiler_params=pltpu.CompilerParams(vmem_limit_bytes=9 * MIB),
        name="bring",
    )(value)


def project(rows_own, rows_other, weights, outs_rows, dtype, most=640):
    rows, depth = rows_own.shape
    width = sum(piece.shape[1] for piece in weights[0][2])
    tile = min(tile_of(piece.shape[1], most) for _, _, pieces in weights for piece in pieces)
    count = len(weights)
    flat = [w for own, _, pieces in weights for w in (own, *pieces)]

    def kernel(a, b, *refs):
        outs = refs[len(flat) :]
        refs = list(refs[: len(flat)])
        for i, (_, start, pieces) in enumerate(weights):
            own, at = refs.pop(0), 0
            for _ in pieces:
                other = refs.pop(0)

                @pl.loop(0, other.shape[1] // tile)
                def _(j, own=own, other=other, at=at, i=i, start=start):
                    there = pl.ds(pl.multiple_of(j * tile, 128), tile)
                    here = pl.ds(pl.multiple_of(start + at + j * tile, 128), tile)
                    to = pl.ds(pl.multiple_of(at + j * tile, 128), tile)
                    total = jnp.dot(a[...], own[:, here], preferred_element_type=F32)
                    total += jnp.dot(b[...], other[:, there], preferred_element_type=F32)
                    row = 0
                    for out, size in zip(outs, outs_rows):
                        out[i, :, to] = total[row : row + size].astype(dtype)
                        row += size

                at += other.shape[1]

    size = jnp.dtype(dtype).itemsize
    return pl.pallas_call(
        kernel,
        out_shape=[jax.ShapeDtypeStruct((count, r, width), dtype) for r in outs_rows],
        in_specs=[VMEM] * (2 + len(flat)),
        out_specs=[VMEM] * len(outs_rows),
        cost_estimate=pl.CostEstimate(
            flops=4 * rows * depth * width * count,
            bytes_accessed=4 * depth * width * count + 4 * rows * depth + rows * width * count * size,
            transcendentals=0,
        ),
        compiler_params=pltpu.CompilerParams(vmem_limit_bytes=LIMIT * MIB),
        name="project",
    )(rows_own, rows_other, *flat)


def add_received(keep, first, second=None, step=16):
    _, s, half = keep[0].shape
    parts = len(first[0])
    spans, at = [], 0
    for v in first[0]:
        both, _, width = v.shape
        for i in range(both):
            spans.append([(len(spans) if both == 1 else 0), i if both == 2 else 0, (at // half + i), at % half, width])
        at += both * width

    def kernel(*refs):
        keeps, refs = refs[:2], refs[2:]
        firsts, refs = (refs[:parts], refs[parts : 2 * parts]), refs[2 * parts :]
        seconds, outs = (refs[:2], refs[2:]) if second else (None, refs)

        def total(chunk, i, at):
            there = pl.ds(at + s if second else at, step)
            here = pl.ds(at, step)
            values = []
            for part, place, of, column, width in spans:
                if of == i:
                    v = keeps[chunk][i, here, column : column + width]
                    v += firsts[chunk][part][place, there, :].astype(F32)
                    if second:
                        v += seconds[chunk][i, here, column : column + width].astype(F32)
                    values.append(v)
            return jnp.concatenate(values, axis=1) if len(values) > 1 else values[0]

        @pl.loop(0, s // step)
        def _(n):
            at = pl.multiple_of(n * step, step)
            for chunk in range(2):
                sums = [total(chunk, i, at) for i in range(2)]
                if second:
                    outs[0][chunk, pl.ds(at, step), :] = (jax.nn.silu(sums[0]) * sums[1]).astype(BF16)
                else:
                    for i in range(2):
                        outs[chunk][i, pl.ds(at, step), :] = sums[i].astype(BF16)

    shape = jax.ShapeDtypeStruct((2, s, half), BF16)
    inputs = [*keep, *first[0], *first[1], *(second or ())]
    return pl.pallas_call(
        kernel,
        out_shape=shape if second else [shape, shape],
        in_specs=[VMEM] * len(inputs),
        out_specs=VMEM if second else [VMEM, VMEM],
        cost_estimate=pl.CostEstimate(
            flops=16 * s * half, bytes_accessed=28 * s * half, transcendentals=2 * s * half if second else 0
        ),
        compiler_params=pltpu.CompilerParams(vmem_limit_bytes=16 * MIB),
        name="add_received",
    )(*inputs)


def down(where, own, other, weight, direct, most=256):
    _, s, half = own[0].shape
    width = weight.shape[1]
    tile = tile_of(width, most)
    count = len(own)

    def kernel(where_ref, *refs):
        pieces = refs[:count], refs[count : 2 * count]
        w, *outs, held, held_other = refs[2 * count :]
        core, place = where_ref[0], where_ref[1]
        for side, to in enumerate((held, held_other)):
            for r, piece in enumerate(pieces[side]):
                if r < 3:
                    to[place ^ r] = piece[...]
                else:
                    to[place ^ 3, r - 3] = piece[...]

        @pl.loop(0, width // tile)
        def _(j):
            columns = pl.ds(pl.multiple_of(j * tile, 128), tile)
            w_own = w[pl.ds(pl.multiple_of(core * half, 128), half), columns]
            w_other = w[pl.ds(pl.multiple_of((1 - core) * half, 128), half), columns]
            total = jnp.dot(held[...].reshape(8 * s, half), w_own, preferred_element_type=F32)
            total += jnp.dot(held_other[...].reshape(8 * s, half), w_other, preferred_element_type=F32)
            total = total.reshape(4, 2, s, tile)
            if direct:
                for i, out in enumerate(outs):
                    out[:, :, columns] = total[(i + 1) % 4].astype(out.dtype)
            else:
                for i in range(2):
                    outs[0][i, :, :, columns] = total[2 * i + 1].astype(BF16)
                    outs[1][i, :, :, columns] = total[2 * i]

    if direct:
        shapes = [jax.ShapeDtypeStruct((2, s, width), d) for d in (BF16, BF16, BF16, F32)]
    else:
        shapes = [jax.ShapeDtypeStruct((2, 2, s, width), d) for d in (BF16, F32)]
    return pl.pallas_call(
        kernel,
        out_shape=shapes,
        in_specs=[SMEM] + [VMEM] * (2 * count + 1),
        out_specs=[VMEM] * len(shapes),
        scratch_shapes=[pltpu.VMEM((4, 2, s, half), BF16)] * 2,
        cost_estimate=pl.CostEstimate(
            flops=32 * s * half * width,
            bytes_accessed=4 * half * width + 32 * s * half + 24 * s * width,
            transcendentals=0,
        ),
        compiler_params=pltpu.CompilerParams(vmem_limit_bytes=LIMIT * MIB),
        name="down",
    )(where, *own, *other, weight)


def chunked(tokens, gate_weight, up_weight, down_weight, shares, direct=None):
    me, z = lax.axis_index("dp"), lax.axis_index("mp")
    core, chip = me % 2, me // 2
    where = jnp.stack([core, z ^ chip, chip])

    def along(axis, bit, value):
        count = lax.axis_size(axis)
        return lax.ppermute(value, axis, [(i, i ^ bit) for i in range(count)])

    def over_core(value):
        return along("dp", 1, value)

    def over_x(value):
        return along("dp", 2, value)

    def over_y(value):
        return along("dp", 4, value)

    pairs, away, near, at = range(len(shares)), [], [], 0
    for s in shares:
        b = at + s
        away.append([(3, at), (1, at), (3, b), (2, b)])
        near.append([(2, at), (1, b), (0, at), (0, b)])
        at += 2 * s
    lists, sizes = [*away, *near], [*shares, *shares]
    count = len(shares)
    groups = [("rowsa", [0]), ("rowsb", [1, count]), ("rowsc", [*range(2, count), *range(count + 1, 2 * count)])]
    rows = [None] * (2 * count)
    for name, members in groups:
        found = gather_rows(where, tokens, [lists[i] for i in members], [sizes[i] for i in members], ROWS if name == groups[0][0] else 8)
        for i, v in zip(members, found):
            rows[i] = v, over_core(v)
    away, near = rows[:count], rows[count:]
    half = gate_weight.shape[1] // 2
    begin = tile_of(half, half // 3)
    weights = []
    for i, w in enumerate((gate_weight, up_weight)):
        own, *other = halves(where, w, (half,) if i else (begin, half - begin), 17 if i else ALONE)
        other = [over_core(v) for v in other]
        weights.append((own, 0, [bring(v) for v in other]))
    (gate, _, pieces), up = weights
    first, keep = [], []
    s = shares[0]
    sums = []
    for w in ((gate, 0, pieces[:1]), (gate, begin, pieces[1:]), up):
        x_first, y_first = project(*away[0], [w], (2 * s, 2 * s), BF16)
        sums.append((over_x(x_first), over_y(y_first)))
    first.append([[v[i] for v in sums] for i in range(2)])
    for p in pairs:
        s = shares[p]
        if p:
            x_first, y_first = project(*away[p], weights, (2 * s, 2 * s), BF16)
            first.append(([over_x(x_first)], [over_y(y_first)]))
        keep.append(project(*near[p], weights, (s,) * 4, F32))

    outs = []
    for p in pairs:
        s = shares[p]
        onward = add_received(keep[p][:2], first[p])
        second = over_y(onward[0]), over_x(onward[1])
        mine = add_received(keep[p][2:], first[p], second)
        from_x, from_y = over_x(mine), over_y(mine)
        own = [mine, from_x, from_y, over_x(from_y[0]), over_y(from_x[1])]
        other = [over_core(v) for v in own]
        *sent, kept = down(where, own, other, down_weight, direct=p == direct)
        if p == direct:
            far = along("mp", 3, sent[2])
            middle = along("mp", 2, sent[1])
            out = kept + along("mp", 1, sent[0]).astype(F32) + middle.astype(F32) + far.astype(F32)
        else:
            got = along("mp", 1, sent[0])
            passed = along("mp", 2, (kept[1] + got[1].astype(F32)).astype(BF16))
            out = kept[0] + got[0].astype(F32) + passed.astype(F32)
        outs.append(out.astype(BF16).reshape(2 * s, -1))
    return jnp.concatenate(outs)


SHARES = (3,4,3,2)


def plain(tokens, gate_weight, up_weight, down_weight):
    group = gate_weight.shape[1]
    both_weights = jnp.concatenate((gate_weight, up_weight), axis=1)
    summed = lax.psum_scatter(
        jnp.dot(tokens, both_weights, preferred_element_type=F32), "dp", scatter_dimension=0, tiled=True
    )
    hidden = (jax.nn.silu(summed[:, :group]) * summed[:, group:]).astype(BF16)
    partial_out = jnp.dot(
        lax.all_gather(hidden, "dp", axis=0, tiled=True), down_weight, preferred_element_type=F32
    )
    mixed = lax.psum_scatter(partial_out, "mp", scatter_dimension=0, tiled=True)
    return mixed.astype(BF16)


def body(tokens, gate_weight, up_weight, down_weight):
    args = tokens, gate_weight, up_weight, down_weight
    if lax.axis_size("dp") == 8 and lax.axis_size("mp") == 4:
        unit = tokens.shape[0] // (8 * sum(SHARES))
        return chunked(*args, tuple(unit * share for share in SHARES))
    return plain(*args)


def solution(mesh):
    in_specs = (P(None, "dp"), P("dp", "mp"), P("dp", "mp"), P("mp", "dp"))
    out_specs = P("mp", "dp")
    return jax.shard_map(body, mesh=mesh, in_specs=in_specs, out_specs=out_specs, check_vma=False)
```

time: 586 us -> 258 us (0.44)
  waiting for transfers between devices: 452 us -> 123 us
  Pallas kernels: 0 us -> 68.5 us
  starting transfers between devices: 0.27 us -> 59.4 us
  local copies, waits for them, and re-layouts: 62.7 us -> 4.88 us
  matrix products: 50.6 us -> 0 us
  between operations: 13.1 us -> 0.53 us
    unnamed x4 -> x0, waiting for transfers between devices: 272 us -> none
    ppermute x0 -> x75, waiting for transfers between devices: none -> 123 us  [along(): return lax.ppermute(value, axis, [(i, i ^ bit) for i in range(count)])]
    reduce_scatter x1 -> x0, waiting for transfers between devices: 111 us -> none  [body(): mixed = lax.psum_scatter(partial_out, 'mp', scatter_dimension=0, tiled=True)]
    all_gather x1 -> x0, waiting for transfers between devices: 68.6 us -> none  [body(): lax.all_gather(hidden, 'dp', axis=0, tiled=True)]
    pallas_call x0 -> x30, Pallas kernels: none -> 68.5 us  [the longest x10 38.6 us: project(): pl.pallas_call(kernel, out_shape=[jax.ShapeDtypeStruct((count, r, width),...]
    ppermute x0 -> x75, starting transfers between devices: none -> 59.4 us  [along(): return lax.ppermute(value, axis, [(i, i ^ bit) for i in range(count)])]
    unnamed x7 -> x10, local copies, waits for them, and re-layouts: 55.8 us -> 4.77 us
    dot_general x2 -> x0, matrix products: 50.6 us -> none  [the longest x1 32.1 us: body(): jnp.dot(tokens, both_weights, preferred_element_type=jnp.float32)]
  transfers between devices with their start and end apart: 3 -> 75, of which waited for: 3 -> 23; matrix products, arithmetic and copies ran while one was open for 0% -> 0% of each run, Pallas kernels for 0% -> 26%
where the time goes in v1:
time: 258 us; the launch traced here: 257 us
  waiting for transfers between devices  123 us (48%)
  Pallas kernels  68.5 us (27%)
  starting transfers between devices  59.4 us (23%)
  local copies, waits for them, and re-layouts  4.88 us (2%)
    ppermute x75, waiting for transfers between devices, along(): return lax.ppermute(value, axis, [(i, i ^ bit) for i in range(count)])  123 us
    ppermute x75, starting transfers between devices, along(): return lax.ppermute(value, axis, [(i, i ^ bit) for i in range(count)])  59.4 us
    pallas_call x10, Pallas kernels, project(): pl.pallas_call(kernel, out_shape=[jax.ShapeDtypeStruct((count, r, width),...  38.6 us
    pallas_call x4, Pallas kernels, down(): pl.pallas_call(kernel, out_shape=shapes, in_specs=[SMEM] + [VMEM] * (2 *...  18.9 us
    pallas_call x3, Pallas kernels, gather_rows(): pl.pallas_call(kernel, out_shape=[jax.ShapeDtypeStruct((len(p) * s, depth...  6.05 us
  transfers between devices with their start and end apart: 75, of which 23 were waited for; matrix products, arithmetic and copies ran while one was open for 0% of the time, Pallas kernels for 26%

profile of v1, /device:TPU:0, one launch (start us, length us, event | category | flops | bytes accessed | tf_op | source)
XLA Modules:
  0.0 257.4 jit_solution(3299664065277515093)
XLA Ops:
  22.5 3.6 %project.19 = (bf16[2,64,1920]{2,1,0:T(8,128)(2,1)S(1)}, bf16[2,64,1920]{2,1,0:T(8,128)(2,1)S(1)}) custom-call(bf16[128,1024]{1,0:T(8,128)(2,1)S(1)} %get-tuple-element.108.a, bf16[128,1024]{1,0:T(8,128)(2,1)S(1)} %collective-permute-done.59.b, bf16[1024,1920]{1,0:T(8,128)(2,1)S(1)} %get-tuple-element.62.refs_0_, bf16[1024,640]{1,0:T(8,128)(2,1)S(1)} %bring.3.refs_1_, ...), custom_call_target="tpu_custom_call" | custom-call | flops 2013265920 | bytes 17235968 | tf_op jit(solution)/shard_map/project/pallas_call | solution.py:135
  32.8 6.0 %project.15 = (bf16[2,128,1920]{2,1,0:T(8,128)(2,1)S(1)}, bf16[2,128,1920]{2,1,0:T(8,128)(2,1)S(1)}) custom-call(bf16[256,1024]{1,0:T(8,128)(2,1)S(1)} %get-tuple-element.84.a, bf16[256,1024]{1,0:T(8,128)(2,1)S(1)} %collective-permute-done.25.b, bf16[1024,1920]{1,0:T(8,128)(2,1)S(1)} %get-tuple-element.62.refs_0_, bf16[1024,640]{1,0:T(8,128)(2,1)S(1)} %bring.3.refs_1_, ...), custom_call_target="tpu_custom_call" | custom-call | flops 4026531840 | bytes 18743296 | tf_op jit(solution)/shard_map/project/pallas_call | solution.py:135
  42.8 7.1 %collective-permute-done.8.refs_5_ = bf16[1,96,640]{2,1,0:T(8,128)(2,1)S(1)} collective-permute-done((bf16[1,96,640]{2,1,0:T(8,128)(2,1)S(1)}, bf16[1,96,640]{2,1,0:T(8,128)(2,1)S(1)}, u32[]{:S(2)}, u32[]{:S(2)}) %collective-permute-start.8) | collective-permute-done | bytes 122912 | tf_op jit(solution)/shard_map/ppermute | solution.py:264
  53.2 4.8 %project.17 = (bf16[2,96,1920]{2,1,0:T(8,128)(2,1)S(1)}, bf16[2,96,1920]{2,1,0:T(8,128)(2,1)S(1)}) custom-call(bf16[192,1024]{1,0:T(8,128)(2,1)S(1)} %get-tuple-element.96.a, bf16[192,1024]{1,0:T(8,128)(2,1)S(1)} %collective-permute-done.42.b, bf16[1024,1920]{1,0:T(8,128)(2,1)S(1)} %get-tuple-element.62.refs_0_, bf16[1024,640]{1,0:T(8,128)(2,1)S(1)} %bring.3.refs_1_, ...), custom_call_target="tpu_custom_call" | custom-call | flops 3019898880 | bytes 17989632 | tf_op jit(solution)/shard_map/project/pallas_call | solution.py:135
  59.0 3.6 %project.18 = (f32[2,32,1920]{2,1,0:T(8,128)S(1)}, f32[2,32,1920]{2,1,0:T(8,128)S(1)}, f32[2,32,1920]{2,1,0:T(8,128)S(1)}, f32[2,32,1920]{2,1,0:T(8,128)S(1)}) custom-call(bf16[128,1024]{1,0:T(8,128)(2,1)S(1)} %get-tuple-element.105.a, bf16[128,1024]{1,0:T(8,128)(2,1)S(1)} %collective-permute-done.58.b, bf16[1024,1920]{1,0:T(8,128)(2,1)S(1)} %get-tuple-element.62.refs_0_, ...), custom_call_target="tpu_custom_call" | custom-call | flops 2013265920 | bytes 18219008 | tf_op jit(solution)/shard_map/project/pallas_call | solution.py:135
  65.9 5.0 %project.10 = (f32[2,48,1920]{2,1,0:T(8,128)S(1)}, f32[2,48,1920]{2,1,0:T(8,128)S(1)}, f32[2,48,1920]{2,1,0:T(8,128)S(1)}, f32[2,48,1920]{2,1,0:T(8,128)S(1)}) custom-call(bf16[192,1024]{1,0:T(8,128)(2,1)S(1)} %get-tuple-element.61.a, bf16[192,1024]{1,0:T(8,128)(2,1)S(1)} %collective-permute-done.b, bf16[1024,1920]{1,0:T(8,128)(2,1)S(1)} %get-tuple-element.62.refs_0_, ...), custom_call_target="tpu_custom_call" | custom-call | flops 3019898880 | bytes 19464192 | tf_op jit(solution)/shard_map/project/pallas_call | solution.py:135
  71.7 11.8 %collective-permute-done.62.refs_4_ = bf16[2,32,1920]{2,1,0:T(8,128)(2,1)S(1)} collective-permute-done((bf16[2,32,1920]{2,1,0:T(8,128)(2,1)S(1)}, bf16[2,32,1920]{2,1,0:T(8,128)(2,1)S(1)}, u32[]{:S(2)}, u32[]{:S(2)}) %collective-permute-start.62) | collective-permute-done | bytes 245792 | tf_op jit(solution)/shard_map/ppermute | solution.py:264
  85.5 6.0 %project.14 = (f32[2,64,1920]{2,1,0:T(8,128)S(1)}, f32[2,64,1920]{2,1,0:T(8,128)S(1)}, f32[2,64,1920]{2,1,0:T(8,128)S(1)}, f32[2,64,1920]{2,1,0:T(8,128)S(1)}) custom-call(bf16[256,1024]{1,0:T(8,128)(2,1)S(1)} %get-tuple-element.81.a, bf16[256,1024]{1,0:T(8,128)(2,1)S(1)} %collective-permute-done.24.b, bf16[1024,1920]{1,0:T(8,128)(2,1)S(1)} %get-tuple-element.62.refs_0_, ...), custom_call_target="tpu_custom_call" | custom-call | flops 4026531840 | bytes 20709376 | tf_op jit(solution)/shard_map/project/pallas_call | solution.py:135
  93.8 4.8 %project.16 = (f32[2,48,1920]{2,1,0:T(8,128)S(1)}, f32[2,48,1920]{2,1,0:T(8,128)S(1)}, f32[2,48,1920]{2,1,0:T(8,128)S(1)}, f32[2,48,1920]{2,1,0:T(8,128)S(1)}) custom-call(bf16[192,1024]{1,0:T(8,128)(2,1)S(1)} %get-tuple-element.93.a, bf16[192,1024]{1,0:T(8,128)(2,1)S(1)} %collective-permute-done.41.b, bf16[1024,1920]{1,0:T(8,128)(2,1)S(1)} %get-tuple-element.62.refs_0_, ...), custom_call_target="tpu_custom_call" | custom-call | flops 3019898880 | bytes 19464192 | tf_op jit(solution)/shard_map/project/pallas_call | solution.py:135
  100.4 11.3 %collective-permute-done.12.refs_9_ = bf16[2,48,1920]{2,1,0:T(8,128)(2,1)S(1)} collective-permute-done((bf16[2,48,1920]{2,1,0:T(8,128)(2,1)S(1)}, bf16[2,48,1920]{2,1,0:T(8,128)(2,1)S(1)}, u32[]{:S(2)}, u32[]{:S(2)}) %collective-permute-start.12) | collective-permute-done | bytes 368672 | tf_op jit(solution)/shard_map/ppermute | solution.py:264
  112.1 7.6 %collective-permute-done.65.refs_2_ = bf16[2,32,1920]{2,1,0:T(8,128)(2,1)S(1)} collective-permute-done((bf16[2,32,1920]{2,1,0:T(8,128)(2,1)S(1)}, bf16[2,32,1920]{2,1,0:T(8,128)(2,1)S(1)}, u32[]{:S(2)}, u32[]{:S(2)}) %collective-permute-start.65) | collective-permute-done | bytes 245792 | tf_op jit(solution)/shard_map/ppermute | solution.py:264
  125.5 5.5 %collective-permute-done.45.refs_4_ = bf16[2,48,1920]{2,1,0:T(8,128)(2,1)S(1)} collective-permute-done((bf16[2,48,1920]{2,1,0:T(8,128)(2,1)S(1)}, bf16[2,48,1920]{2,1,0:T(8,128)(2,1)S(1)}, u32[]{:S(2)}, u32[]{:S(2)}) %collective-permute-start.45) | collective-permute-done | bytes 368672 | tf_op jit(solution)/shard_map/ppermute | solution.py:264
  132.7 5.2 %collective-permute-done.14.refs_2_ = bf16[2,48,1920]{2,1,0:T(8,128)(2,1)S(1)} collective-permute-done((bf16[2,48,1920]{2,1,0:T(8,128)(2,1)S(1)}, bf16[2,48,1920]{2,1,0:T(8,128)(2,1)S(1)}, u32[]{:S(2)}, u32[]{:S(2)}) %collective-permute-start.14) | collective-permute-done | bytes 368672 | tf_op jit(solution)/shard_map/ppermute | solution.py:264
  145.5 3.5 %down.7 = (bf16[2,2,32,1024]{3,2,1,0:T(8,128)(2,1)S(1)}, f32[2,2,32,1024]{3,2,1,0:T(8,128)S(1)}) custom-call(s32[3]{0:T(128)S(1)} %pad_add_fusion.where_ref, bf16[2,32,1920]{2,1,0:T(8,128)(2,1)S(1)} %add_received.15.refs_0_, bf16[2,32,1920]{2,1,0:T(8,128)(2,1)S(1)} %collective-permute-done.64.refs_1_, ...), custom_call_target="tpu_custom_call" | custom-call | flops 2013265920 | bytes 10616832 | tf_op jit(solution)/shard_map/down/pallas_call | solution.py:241
  149.1 5.8 %collective-permute-done.28.refs_4_ = bf16[2,64,1920]{2,1,0:T(8,128)(2,1)S(1)} collective-permute-done((bf16[2,64,1920]{2,1,0:T(8,128)(2,1)S(1)}, bf16[2,64,1920]{2,1,0:T(8,128)(2,1)S(1)}, u32[]{:S(2)}, u32[]{:S(2)}) %collective-permute-start.28) | collective-permute-done | bytes 491552 | tf_op jit(solution)/shard_map/ppermute | solution.py:264
  156.4 3.5 %collective-permute-done.48.refs_2_ = bf16[2,48,1920]{2,1,0:T(8,128)(2,1)S(1)} collective-permute-done((bf16[2,48,1920]{2,1,0:T(8,128)(2,1)S(1)}, bf16[2,48,1920]{2,1,0:T(8,128)(2,1)S(1)}, u32[]{:S(2)}, u32[]{:S(2)}) %collective-permute-start.48) | collective-permute-done | bytes 368672 | tf_op jit(solution)/shard_map/ppermute | solution.py:264
  167.0 8.7 %collective-permute-done.16.refs_4_ = bf16[48,1920]{1,0:T(8,128)(2,1)S(1)} collective-permute-done((bf16[48,1920]{1,0:T(8,128)(2,1)S(1)}, bf16[48,1920]{1,0:T(8,128)(2,1)S(1)}, u32[]{:S(2)}, u32[]{:S(2)}) %collective-permute-start.16) | collective-permute-done | bytes 184352 | tf_op jit(solution)/shard_map/ppermute | solution.py:264
  180.5 4.3 %collective-permute-done.49.refs_3_ = bf16[48,1920]{1,0:T(8,128)(2,1)S(1)} collective-permute-done((bf16[48,1920]{1,0:T(8,128)(2,1)S(1)}, bf16[48,1920]{1,0:T(8,128)(2,1)S(1)}, u32[]{:S(2)}, u32[]{:S(2)}) %collective-permute-start.49) | collective-permute-done | bytes 184352 | tf_op jit(solution)/shard_map/ppermute | solution.py:264
  188.3 4.7 %down.4 = (bf16[2,2,48,1024]{3,2,1,0:T(8,128)(2,1)S(1)}, f32[2,2,48,1024]{3,2,1,0:T(8,128)S(1)}) custom-call(s32[3]{0:T(128)S(1)} %pad_add_fusion.where_ref, bf16[2,48,1920]{2,1,0:T(8,128)(2,1)S(1)} %add_received.9.refs_0_, bf16[2,48,1920]{2,1,0:T(8,128)(2,1)S(1)} %collective-permute-done.13.refs_1_, ...), custom_call_target="tpu_custom_call" | custom-call | flops 3019898880 | bytes 11993088 | tf_op jit(solution)/shard_map/down/pallas_call | solution.py:241
  194.7 4.9 %down.6 = (bf16[2,2,48,1024]{3,2,1,0:T(8,128)(2,1)S(1)}, f32[2,2,48,1024]{3,2,1,0:T(8,128)S(1)}) custom-call(s32[3]{0:T(128)S(1)} %pad_add_fusion.where_ref, bf16[2,48,1920]{2,1,0:T(8,128)(2,1)S(1)} %add_received.13.refs_0_, bf16[2,48,1920]{2,1,0:T(8,128)(2,1)S(1)} %collective-permute-done.47.refs_1_, ...), custom_call_target="tpu_custom_call" | custom-call | flops 3019898880 | bytes 11993088 | tf_op jit(solution)/shard_map/down/pallas_call | solution.py:241
  204.3 5.8 %down.5 = (bf16[2,2,64,1024]{3,2,1,0:T(8,128)(2,1)S(1)}, f32[2,2,64,1024]{3,2,1,0:T(8,128)S(1)}) custom-call(s32[3]{0:T(128)S(1)} %pad_add_fusion.where_ref, bf16[2,64,1920]{2,1,0:T(8,128)(2,1)S(1)} %add_received.11.refs_0_, bf16[2,64,1920]{2,1,0:T(8,128)(2,1)S(1)} %collective-permute-done.30.refs_1_, ...), custom_call_target="tpu_custom_call" | custom-call | flops 4026531840 | bytes 13369344 | tf_op jit(solution)/shard_map/down/pallas_call | solution.py:241
  216.5 10.6 %collective-permute-done.56 = bf16[2,2,48,1024]{3,2,1,0:T(8,128)(2,1)S(1)} collective-permute-done((bf16[2,2,48,1024]{3,2,1,0:T(8,128)(2,1)S(1)}, bf16[2,2,48,1024]{3,2,1,0:T(8,128)(2,1)S(1)}, u32[]{:S(2)}, u32[]{:S(2)}) %collective-permute-start.56) | collective-permute-done | bytes 393248 | tf_op jit(solution)/shard_map/ppermute | solution.py:264
  228.3 13.8 %collective-permute-done.39 = bf16[2,2,64,1024]{3,2,1,0:T(8,128)(2,1)S(1)} collective-permute-done((bf16[2,2,64,1024]{3,2,1,0:T(8,128)(2,1)S(1)}, bf16[2,2,64,1024]{3,2,1,0:T(8,128)(2,1)S(1)}, u32[]{:S(2)}, u32[]{:S(2)}) %collective-permute-start.39) | collective-permute-done | bytes 524320 | tf_op jit(solution)/shard_map/ppermute | solution.py:264
  242.8 13.5 %collective-permute-done.40 = bf16[2,64,1024]{2,1,0:T(8,128)(2,1)S(1)} collective-permute-done((bf16[2,64,1024]{2,1,0:T(8,128)(2,1)S(1)}, bf16[2,64,1024]{2,1,0:T(8,128)(2,1)S(1)}, u32[]{:S(2)}, u32[]{:S(2)}) %collective-permute-start.40) | collective-permute-done | bytes 262176 | tf_op jit(solution)/shard_map/ppermute | solution.py:264
  (185 shorter events, 95.5 us)
Async XLA Ops:
  28.8 21.2 %collective-permute-start.6 = (bf16[1,96,1280]{2,1,0:T(8,128)(2,1)S(1)}, bf16[1,96,1280]{2,1,0:T(8,128)(2,1)S(1)}, u32[]{:S(2)}, u32[]{:S(2)}) collective-permute-start(bf16[1,96,1280]{2,1,0:T(8,128)(2,1)S(1)} %get-tuple-element.70), channel_id=1, source_target_pairs={{0,8},{4,12},{8,0},{12,4},{16,24},{20,28},{24,16},{28,20},{1,9},{5... | collective-permute-start | bytes 737288 | tf_op jit(solution)/shard_map/ppermute | solution.py:264
  28.9 22.8 %collective-permute-start.9 = (bf16[1,96,1280]{2,1,0:T(8,128)(2,1)S(1)}, bf16[1,96,1280]{2,1,0:T(8,128)(2,1)S(1)}, u32[]{:S(2)}, u32[]{:S(2)}) collective-permute-start(bf16[1,96,1280]{2,1,0:T(8,128)(2,1)S(1)} %get-tuple-element.73), channel_id=1, source_target_pairs={{0,16},{4,20},{8,24},{12,28},{16,0},{20,4},{24,8},{28,12},{1,17},{... | collective-permute-start | bytes 737288 | tf_op jit(solution)/shard_map/ppermute | solution.py:264
  30.8 27.2 %collective-permute-start.60 = (bf16[2,64,1920]{2,1,0:T(8,128)(2,1)S(1)}, bf16[2,64,1920]{2,1,0:T(8,128)(2,1)S(1)}, u32[]{:S(2)}, u32[]{:S(2)}) collective-permute-start(bf16[2,64,1920]{2,1,0:T(8,128)(2,1)S(1)} %get-tuple-element.109), channel_id=1, source_target_pairs={{0,8},{4,12},{8,0},{12,4},{16,24},{20,28},{24,16},{28,20},{1,9},{5... | collective-permute-start | bytes 1474568 | tf_op jit(solution)/shard_map/ppermute | solution.py:264
  32.3 26.3 %collective-permute-start.61 = (bf16[2,64,1920]{2,1,0:T(8,128)(2,1)S(1)}, bf16[2,64,1920]{2,1,0:T(8,128)(2,1)S(1)}, u32[]{:S(2)}, u32[]{:S(2)}) collective-permute-start(bf16[2,64,1920]{2,1,0:T(8,128)(2,1)S(1)} %get-tuple-element.110), channel_id=1, source_target_pairs={{0,16},{4,20},{8,24},{12,28},{16,0},{20,4},{24,8},{28,12},{1,17},{... | collective-permute-start | bytes 1474568 | tf_op jit(solution)/shard_map/ppermute | solution.py:264
  50.0 21.1 %collective-permute-start.24 = (bf16[256,1024]{1,0:T(8,128)(2,1)S(1)}, bf16[256,1024]{1,0:T(8,128)(2,1)S(1)}, u32[]{:S(2)}, u32[]{:S(2)}) collective-permute-start(bf16[256,1024]{1,0:T(8,128)(2,1)S(1)} %get-tuple-element.81.a), channel_id=1, source_target_pairs={{0,4},{4,0},{8,12},{12,8},{16,20},{20,16},{24,28},{28,24},{1,5},{5... | collective-permute-start | bytes 1572872 | tf_op jit(solution)/shard_map/ppermute | solution.py:264
  58.0 33.7 %collective-permute-start.43 = (bf16[2,96,1920]{2,1,0:T(8,128)(2,1)S(1)}, bf16[2,96,1920]{2,1,0:T(8,128)(2,1)S(1)}, u32[]{:S(2)}, u32[]{:S(2)}) collective-permute-start(bf16[2,96,1920]{2,1,0:T(8,128)(2,1)S(1)} %get-tuple-element.97), channel_id=1, source_target_pairs={{0,8},{4,12},{8,0},{12,4},{16,24},{20,28},{24,16},{28,20},{1,9},{5... | collective-permute-start | bytes 2211848 | tf_op jit(solution)/shard_map/ppermute | solution.py:264
  58.6 33.5 %collective-permute-start.44 = (bf16[2,96,1920]{2,1,0:T(8,128)(2,1)S(1)}, bf16[2,96,1920]{2,1,0:T(8,128)(2,1)S(1)}, u32[]{:S(2)}, u32[]{:S(2)}) collective-permute-start(bf16[2,96,1920]{2,1,0:T(8,128)(2,1)S(1)} %get-tuple-element.98), channel_id=1, source_target_pairs={{0,16},{4,20},{8,24},{12,28},{16,0},{20,4},{24,8},{28,12},{1,17},{... | collective-permute-start | bytes 2211848 | tf_op jit(solution)/shard_map/ppermute | solution.py:264
  62.7 20.8 %collective-permute-start.62 = (bf16[2,32,1920]{2,1,0:T(8,128)(2,1)S(1)}, bf16[2,32,1920]{2,1,0:T(8,128)(2,1)S(1)}, u32[]{:S(2)}, u32[]{:S(2)}) collective-permute-start(bf16[2,32,1920]{2,1,0:T(8,128)(2,1)S(1)} %get-tuple-element.113), channel_id=1, source_target_pairs={{0,16},{4,20},{8,24},{12,28},{16,0},{20,4},{24,8},{28,12},{1,17},{... | collective-permute-start | bytes 737288 | tf_op jit(solution)/shard_map/ppermute | solution.py:264
  64.4 20.6 %collective-permute-start.63 = (bf16[2,32,1920]{2,1,0:T(8,128)(2,1)S(1)}, bf16[2,32,1920]{2,1,0:T(8,128)(2,1)S(1)}, u32[]{:S(2)}, u32[]{:S(2)}) collective-permute-start(bf16[2,32,1920]{2,1,0:T(8,128)(2,1)S(1)} %get-tuple-element.114), channel_id=1, source_target_pairs={{0,8},{4,12},{8,0},{12,4},{16,24},{20,28},{24,16},{28,20},{1,9},{5... | collective-permute-start | bytes 737288 | tf_op jit(solution)/shard_map/ppermute | solution.py:264
  71.1 50.7 %collective-permute-start.26 = (bf16[2,128,1920]{2,1,0:T(8,128)(2,1)S(1)}, bf16[2,128,1920]{2,1,0:T(8,128)(2,1)S(1)}, u32[]{:S(2)}, u32[]{:S(2)}) collective-permute-start(bf16[2,128,1920]{2,1,0:T(8,128)(2,1)S(1)} %get-tuple-element.85), channel_id=1, source_target_pairs={{0,8},{4,12},{8,0},{12,4},{16,24},{20,28},{24,16},{28,20},{1,9},{5... | collective-permute-start | bytes 2949128 | tf_op jit(solution)/shard_map/ppermute | solution.py:264
  85.0 26.7 %collective-permute-start.12 = (bf16[2,48,1920]{2,1,0:T(8,128)(2,1)S(1)}, bf16[2,48,1920]{2,1,0:T(8,128)(2,1)S(1)}, u32[]{:S(2)}, u32[]{:S(2)}) collective-permute-start(bf16[2,48,1920]{2,1,0:T(8,128)(2,1)S(1)} %get-tuple-element.78), channel_id=1, source_target_pairs={{0,8},{4,12},{8,0},{12,4},{16,24},{20,28},{24,16},{28,20},{1,9},{5... | collective-permute-start | bytes 1105928 | tf_op jit(solution)/shard_map/ppermute | solution.py:264
  91.7 31.4 %collective-permute-start.27 = (bf16[2,128,1920]{2,1,0:T(8,128)(2,1)S(1)}, bf16[2,128,1920]{2,1,0:T(8,128)(2,1)S(1)}, u32[]{:S(2)}, u32[]{:S(2)}) collective-permute-start(bf16[2,128,1920]{2,1,0:T(8,128)(2,1)S(1)} %get-tuple-element.86), channel_id=1, source_target_pairs={{0,16},{4,20},{8,24},{12,28},{16,0},{20,4},{24,8},{28,12},{1,17},{... | collective-permute-start | bytes 2949128 | tf_op jit(solution)/shard_map/ppermute | solution.py:264
  92.1 27.5 %collective-permute-start.65 = (bf16[2,32,1920]{2,1,0:T(8,128)(2,1)S(1)}, bf16[2,32,1920]{2,1,0:T(8,128)(2,1)S(1)}, u32[]{:S(2)}, u32[]{:S(2)}) collective-permute-start(bf16[2,32,1920]{2,1,0:T(8,128)(2,1)S(1)} %add_received.15.refs_0_), channel_id=1, source_target_pairs={{0,16},{4,20},{8,24},{12,28},{16,0},{20,4},{24,8},{28,12},{1,17},{... | collective-permute-start | bytes 737288 | tf_op jit(solution)/shard_map/ppermute | solution.py:264
  98.8 22.3 %collective-permute-start.64 = (bf16[2,32,1920]{2,1,0:T(8,128)(2,1)S(1)}, bf16[2,32,1920]{2,1,0:T(8,128)(2,1)S(1)}, u32[]{:S(2)}, u32[]{:S(2)}) collective-permute-start(bf16[2,32,1920]{2,1,0:T(8,128)(2,1)S(1)} %add_received.15.refs_0_), channel_id=1, source_target_pairs={{0,8},{4,12},{8,0},{12,4},{16,24},{20,28},{24,16},{28,20},{1,9},{5... | collective-permute-start | bytes 737288 | tf_op jit(solution)/shard_map/ppermute | solution.py:264
  123.2 18.7 %collective-permute-start.13 = (bf16[2,48,1920]{2,1,0:T(8,128)(2,1)S(1)}, bf16[2,48,1920]{2,1,0:T(8,128)(2,1)S(1)}, u32[]{:S(2)}, u32[]{:S(2)}) collective-permute-start(bf16[2,48,1920]{2,1,0:T(8,128)(2,1)S(1)} %add_received.9.refs_0_), channel_id=1, source_target_pairs={{0,8},{4,12},{8,0},{12,4},{16,24},{20,28},{24,16},{28,20},{1,9},{5... | collective-permute-start | bytes 1105928 | tf_op jit(solution)/shard_map/ppermute | solution.py:264
  124.1 16.7 %collective-permute-start.66 = (bf16[32,1920]{1,0:T(8,128)(2,1)S(1)}, bf16[32,1920]{1,0:T(8,128)(2,1)S(1)}, u32[]{:S(2)}, u32[]{:S(2)}) collective-permute-start(bf16[32,1920]{1,0:T(8,128)(2,1)S(1)} %slice_bitcast_fusion.7), channel_id=1, source_target_pairs={{0,8},{4,12},{8,0},{12,4},{16,24},{20,28},{24,16},{28,20},{1,9},{5... | collective-permute-start | bytes 368648 | tf_op jit(solution)/shard_map/ppermute | solution.py:264
  142.4 17.5 %collective-permute-start.48 = (bf16[2,48,1920]{2,1,0:T(8,128)(2,1)S(1)}, bf16[2,48,1920]{2,1,0:T(8,128)(2,1)S(1)}, u32[]{:S(2)}, u32[]{:S(2)}) collective-permute-start(bf16[2,48,1920]{2,1,0:T(8,128)(2,1)S(1)} %add_received.13.refs_0_), channel_id=1, source_target_pairs={{0,16},{4,20},{8,24},{12,28},{16,0},{20,4},{24,8},{28,12},{1,17},{... | collective-permute-start | bytes 1105928 | tf_op jit(solution)/shard_map/ppermute | solution.py:264
  143.6 18.0 %collective-permute-start.17 = (bf16[2,48,1920]{2,1,0:T(8,128)(2,1)S(1)}, bf16[2,48,1920]{2,1,0:T(8,128)(2,1)S(1)}, u32[]{:S(2)}, u32[]{:S(2)}) collective-permute-start(bf16[2,48,1920]{2,1,0:T(8,128)(2,1)S(1)} %add_received.9.refs_0_), channel_id=1, source_target_pairs={{0,4},{4,0},{8,12},{12,8},{16,20},{20,16},{24,28},{28,24},{1,5},{5... | collective-permute-start | bytes 1105928 | tf_op jit(solution)/shard_map/ppermute | solution.py:264
  143.7 19.3 %collective-permute-start.47 = (bf16[2,48,1920]{2,1,0:T(8,128)(2,1)S(1)}, bf16[2,48,1920]{2,1,0:T(8,128)(2,1)S(1)}, u32[]{:S(2)}, u32[]{:S(2)}) collective-permute-start(bf16[2,48,1920]{2,1,0:T(8,128)(2,1)S(1)} %add_received.13.refs_0_), channel_id=1, source_target_pairs={{0,8},{4,12},{8,0},{12,4},{16,24},{20,28},{24,16},{28,20},{1,9},{5... | collective-permute-start | bytes 1105928 | tf_op jit(solution)/shard_map/ppermute | solution.py:264
  154.9 20.8 %collective-permute-start.51 = (bf16[2,48,1920]{2,1,0:T(8,128)(2,1)S(1)}, bf16[2,48,1920]{2,1,0:T(8,128)(2,1)S(1)}, u32[]{:S(2)}, u32[]{:S(2)}) collective-permute-start(bf16[2,48,1920]{2,1,0:T(8,128)(2,1)S(1)} %add_received.13.refs_0_), channel_id=1, source_target_pairs={{0,4},{4,0},{8,12},{12,8},{16,20},{20,16},{24,28},{28,24},{1,5},{5... | collective-permute-start | bytes 1105928 | tf_op jit(solution)/shard_map/ppermute | solution.py:264
  163.0 16.9 %collective-permute-start.30 = (bf16[2,64,1920]{2,1,0:T(8,128)(2,1)S(1)}, bf16[2,64,1920]{2,1,0:T(8,128)(2,1)S(1)}, u32[]{:S(2)}, u32[]{:S(2)}) collective-permute-start(bf16[2,64,1920]{2,1,0:T(8,128)(2,1)S(1)} %add_received.11.refs_0_), channel_id=1, source_target_pairs={{0,8},{4,12},{8,0},{12,4},{16,24},{20,28},{24,16},{28,20},{1,9},{5... | collective-permute-start | bytes 1474568 | tf_op jit(solution)/shard_map/ppermute | solution.py:264
  203.2 23.9 %collective-permute-start.56 = (bf16[2,2,48,1024]{3,2,1,0:T(8,128)(2,1)S(1)}, bf16[2,2,48,1024]{3,2,1,0:T(8,128)(2,1)S(1)}, u32[]{:S(2)}, u32[]{:S(2)}) collective-permute-start(bf16[2,2,48,1024]{3,2,1,0:T(8,128)(2,1)S(1)} %get-tuple-element.104), channel_id=1, source_target_pairs={{0,1},{1,0},{2,3},{3,2},{4,5},{5,4},{6,7},{7,6},{8,9},{9,8},{10,11... | collective-permute-start | bytes 1179656 | tf_op jit(solution)/shard_map/ppermute | solution.py:264
  210.1 32.0 %collective-permute-start.39 = (bf16[2,2,64,1024]{3,2,1,0:T(8,128)(2,1)S(1)}, bf16[2,2,64,1024]{3,2,1,0:T(8,128)(2,1)S(1)}, u32[]{:S(2)}, u32[]{:S(2)}) collective-permute-start(bf16[2,2,64,1024]{3,2,1,0:T(8,128)(2,1)S(1)} %get-tuple-element.92), channel_id=1, source_target_pairs={{0,1},{1,0},{2,3},{3,2},{4,5},{5,4},{6,7},{7,6},{8,9},{9,8},{10,11... | collective-permute-start | bytes 1572872 | tf_op jit(solution)/shard_map/ppermute | solution.py:264
  214.5 28.2 %collective-permute-start.23 = (bf16[2,48,1024]{2,1,0:T(8,128)(2,1)S(1)}, bf16[2,48,1024]{2,1,0:T(8,128)(2,1)S(1)}, u32[]{:S(2)}, u32[]{:S(2)}) collective-permute-start(bf16[2,48,1024]{2,1,0:T(8,128)(2,1)S(1)} %fusion.5), channel_id=1, source_target_pairs={{0,2},{1,3},{2,0},{3,1},{4,6},{5,7},{6,4},{7,5},{8,10},{9,11},{10,... | collective-permute-start | bytes 589832 | tf_op jit(solution)/shard_map/ppermute | solution.py:264
  (56 other events, 590.9 us)

commit v2 on v1

--- a/solution.py
+++ b/solution.py
@@ -9,18 +9,17 @@
 F32, BF16 = jnp.float32, jnp.bfloat16
 MIB = 1 << 20
 ANY = pl.BlockSpec(memory_space=pl.ANY)
+HBM = pl.BlockSpec(memory_space=pltpu.HBM)
 VMEM = pl.BlockSpec(memory_space=pltpu.VMEM)
 SMEM = pl.BlockSpec(memory_space=pltpu.SMEM)
 LIMIT = 16
-ALONE = 17
-ROWS = 8
 
 
 def tile_of(extent, most):
     return max(t for t in range(128, min(extent, most) + 1, 128) if extent % t == 0)
 
 
-def gather_rows(where, tokens, lists, sizes, limit=8):
+def gather_rows(where, tokens, lists, sizes):
     depth = tokens.shape[1]
     block = tokens.shape[0] // 4
     count = sum(map(len, lists))
@@ -44,20 +43,17 @@
     return pl.pallas_call(
         kernel,
         out_shape=[jax.ShapeDtypeStruct((len(p) * s, depth), BF16) for p, s in zip(lists, sizes)],
-        in_specs=[SMEM, ANY],
+        in_specs=[SMEM, HBM],
         out_specs=[VMEM] * len(lists),
         scratch_shapes=[pltpu.SemaphoreType.DMA((count,))],
         cost_estimate=pl.CostEstimate(flops=0, bytes_accessed=4 * tokens.size, transcendentals=0),
-        compiler_params=pltpu.CompilerParams(vmem_limit_bytes=limit * MIB),
+        compiler_params=pltpu.CompilerParams(vmem_limit_bytes=8 * MIB),
         name="gather_rows",
     )(where, tokens)
 
 
-def halves(where, weight, cuts, limit):
+def columns_of(where, weight, spans, limit=17):
     depth, half = weight.shape[0], weight.shape[1] // 2
-    spans = [(0, 0, half)]
-    for size in cuts:
-        spans.append((1, sum(size for side, _, size in spans if side), size))
 
     def kernel(where_ref, w, *refs):
         sems = refs[-1]
@@ -75,12 +71,14 @@
     return pl.pallas_call(
         kernel,
         out_shape=[jax.ShapeDtypeStruct((depth, size), BF16) for _, _, size in spans],
-        in_specs=[SMEM, ANY],
+        in_specs=[SMEM, HBM],
         out_specs=[VMEM] * len(spans),
         scratch_shapes=[pltpu.SemaphoreType.DMA((len(spans),))],
-        cost_estimate=pl.CostEstimate(flops=0, bytes_accessed=8 * depth * half, transcendentals=0),
+        cost_estimate=pl.CostEstimate(
+            flops=0, bytes_accessed=4 * depth * sum(size for _, _, size in spans), transcendentals=0
+        ),
         compiler_params=pltpu.CompilerParams(vmem_limit_bytes=limit * MIB),
-        name="halves",
+        name="columns_of",
     )(where, weight)
 
 
@@ -254,7 +252,7 @@
     )(where, *own, *other, weight)
 
 
-def chunked(tokens, gate_weight, up_weight, down_weight, shares, direct=None):
+def chunked(tokens, gate_weight, up_weight, down_weight, shares):
     me, z = lax.axis_index("dp"), lax.axis_index("mp")
     core, chip = me % 2, me // 2
     where = jnp.stack([core, z ^ chip, chip])
@@ -280,10 +278,10 @@
         at += 2 * s
     lists, sizes = [*away, *near], [*shares, *shares]
     count = len(shares)
-    groups = [("rowsa", [0]), ("rowsb", [1, count]), ("rowsc", [*range(2, count), *range(count + 1, 2 * count)])]
+    groups = [[0], [1, count], [*range(2, count), *range(count + 1, 2 * count)]]
     rows = [None] * (2 * count)
-    for name, members in groups:
-        found = gather_rows(where, tokens, [lists[i] for i in members], [sizes[i] for i in members], ROWS if name == groups[0][0] else 8)
+    for members in groups:
+        found = gather_rows(where, tokens, [lists[i] for i in members], [sizes[i] for i in members])
         for i, v in zip(members, found):
             rows[i] = v, over_core(v)
     away, near = rows[:count], rows[count:]
@@ -291,8 +289,12 @@
     begin = tile_of(half, half // 3)
     weights = []
     for i, w in enumerate((gate_weight, up_weight)):
-        own, *other = halves(where, w, (half,) if i else (begin, half - begin), 17 if i else ALONE)
-        other = [over_core(v) for v in other]
+        other = []
+        if not i:
+            other += columns_of(where, w, [(1, 0, begin)])
+        at = sum(v.shape[1] for v in other)
+        own, rest = columns_of(where, w, [(0, 0, half), (1, at, half - at)])
+        other = [over_core(v) for v in [*other, rest]]
         weights.append((own, 0, [bring(v) for v in other]))
     (gate, _, pieces), up = weights
     first, keep = [], []
@@ -318,8 +320,8 @@
         from_x, from_y = over_x(mine), over_y(mine)
         own = [mine, from_x, from_y, over_x(from_y[0]), over_y(from_x[1])]
         other = [over_core(v) for v in own]
-        *sent, kept = down(where, own, other, down_weight, direct=p == direct)
-        if p == direct:
+        *sent, kept = down(where, own, other, down_weight, direct=p in DIRECT)
+        if p in DIRECT:
             far = along("mp", 3, sent[2])
             middle = along("mp", 2, sent[1])
             out = kept + along("mp", 1, sent[0]).astype(F32) + middle.astype(F32) + far.astype(F32)
@@ -331,7 +333,8 @@
     return jnp.concatenate(outs)
 
 
-SHARES = (3,4,3,2)
+SHARES = (3, 4, 3, 2)
+DIRECT = (2, 3)
 
 
 def plain(tokens, gate_weight, up_weight, down_weight):

time: 258 us -> 252 us (0.977)
  waiting for transfers between devices: 123 us -> 113 us
  starting transfers between devices: 59.4 us -> 62.2 us
    ppermute x75 -> x77, waiting for transfers between devices: 123 us -> 113 us  [along(): return lax.ppermute(value, axis, [(i, i ^ bit) for i in range(count)])]
    ppermute x75 -> x77, starting transfers between devices: 59.4 us -> 62.2 us  [along(): return lax.ppermute(value, axis, [(i, i ^ bit) for i in range(count)])]
  transfers between devices with their start and end apart: 75 -> 77, of which waited for: 23 -> 24; matrix products, arithmetic and copies ran while one was open for 0% -> 0% of each run, Pallas kernels for 26% -> 27%
where the time goes in v2:
time: 252 us
  waiting for transfers between devices  113 us (45%)
  Pallas kernels  69.1 us (27%)
  starting transfers between devices  62.2 us (25%)
  local copies, waits for them, and re-layouts  5.45 us (2%)
    ppermute x77, waiting for transfers between devices, along(): return lax.ppermute(value, axis, [(i, i ^ bit) for i in range(count)])  113 us
    ppermute x77, starting transfers between devices, along(): return lax.ppermute(value, axis, [(i, i ^ bit) for i in range(count)])  62.2 us
    pallas_call x10, Pallas kernels, project(): pl.pallas_call(kernel, out_shape=[jax.ShapeDtypeStruct((count, r, width),...  38.6 us
    pallas_call x4, Pallas kernels, down(): pl.pallas_call(kernel, out_shape=shapes, in_specs=[SMEM] + [VMEM] * (2 *...  19 us
    pallas_call x3, Pallas kernels, gather_rows(): pl.pallas_call(kernel, out_shape=[jax.ShapeDtypeStruct((len(p) * s, depth...  6.05 us
    unnamed x10, local copies, waits for them, and re-layouts  5.34 us
  transfers between devices with their start and end apart: 77, of which 24 were waited for; matrix products, arithmetic and copies ran while one was open for 0% of the time, Pallas kernels for 27%

profile of v2, /device:TPU:0, one launch (start us, length us, event | category | flops | bytes accessed | tf_op | source)
XLA Modules:
  0.0 252.2 jit_solution(2347690510940589094)
XLA Ops:
  22.5 3.6 %project.19 = (bf16[2,64,1920]{2,1,0:T(8,128)(2,1)S(1)}, bf16[2,64,1920]{2,1,0:T(8,128)(2,1)S(1)}) custom-call(bf16[128,1024]{1,0:T(8,128)(2,1)S(1)} %get-tuple-element.112.a, bf16[128,1024]{1,0:T(8,128)(2,1)S(1)} %collective-permute-done.60.b, bf16[1024,1920]{1,0:T(8,128)(2,1)S(1)} %get-tuple-element.65.refs_0_, bf16[1024,640]{1,0:T(8,128)(2,1)S(1)} %bring.3.refs_1_, ...), custom_call_target="tpu_custom_call" | custom-call | flops 2013265920 | bytes 17235968 | tf_op jit(solution)/shard_map/project/pallas_call | solution.py:133
  32.8 6.0 %project.15 = (bf16[2,128,1920]{2,1,0:T(8,128)(2,1)S(1)}, bf16[2,128,1920]{2,1,0:T(8,128)(2,1)S(1)}) custom-call(bf16[256,1024]{1,0:T(8,128)(2,1)S(1)} %get-tuple-element.86.a, bf16[256,1024]{1,0:T(8,128)(2,1)S(1)} %collective-permute-done.25.b, bf16[1024,1920]{1,0:T(8,128)(2,1)S(1)} %get-tuple-element.65.refs_0_, bf16[1024,640]{1,0:T(8,128)(2,1)S(1)} %bring.3.refs_1_, ...), custom_call_target="tpu_custom_call" | custom-call | flops 4026531840 | bytes 18743296 | tf_op jit(solution)/shard_map/project/pallas_call | solution.py:133
  42.8 7.2 %collective-permute-done.8.refs_5_ = bf16[1,96,640]{2,1,0:T(8,128)(2,1)S(1)} collective-permute-done((bf16[1,96,640]{2,1,0:T(8,128)(2,1)S(1)}, bf16[1,96,640]{2,1,0:T(8,128)(2,1)S(1)}, u32[]{:S(2)}, u32[]{:S(2)}) %collective-permute-start.8) | collective-permute-done | bytes 122912 | tf_op jit(solution)/shard_map/ppermute | solution.py:262
  53.1 4.8 %project.17 = (bf16[2,96,1920]{2,1,0:T(8,128)(2,1)S(1)}, bf16[2,96,1920]{2,1,0:T(8,128)(2,1)S(1)}) custom-call(bf16[192,1024]{1,0:T(8,128)(2,1)S(1)} %get-tuple-element.98.a, bf16[192,1024]{1,0:T(8,128)(2,1)S(1)} %collective-permute-done.42.b, bf16[1024,1920]{1,0:T(8,128)(2,1)S(1)} %get-tuple-element.65.refs_0_, bf16[1024,640]{1,0:T(8,128)(2,1)S(1)} %bring.3.refs_1_, ...), custom_call_target="tpu_custom_call" | custom-call | flops 3019898880 | bytes 17989632 | tf_op jit(solution)/shard_map/project/pallas_call | solution.py:133
  58.9 3.6 %project.18 = (f32[2,32,1920]{2,1,0:T(8,128)S(1)}, f32[2,32,1920]{2,1,0:T(8,128)S(1)}, f32[2,32,1920]{2,1,0:T(8,128)S(1)}, f32[2,32,1920]{2,1,0:T(8,128)S(1)}) custom-call(bf16[128,1024]{1,0:T(8,128)(2,1)S(1)} %get-tuple-element.109.a, bf16[128,1024]{1,0:T(8,128)(2,1)S(1)} %collective-permute-done.59.b, bf16[1024,1920]{1,0:T(8,128)(2,1)S(1)} %get-tuple-element.65.refs_0_, ...), custom_call_target="tpu_custom_call" | custom-call | flops 2013265920 | bytes 18219008 | tf_op jit(solution)/shard_map/project/pallas_call | solution.py:133
  65.9 5.0 %project.10 = (f32[2,48,1920]{2,1,0:T(8,128)S(1)}, f32[2,48,1920]{2,1,0:T(8,128)S(1)}, f32[2,48,1920]{2,1,0:T(8,128)S(1)}, f32[2,48,1920]{2,1,0:T(8,128)S(1)}) custom-call(bf16[192,1024]{1,0:T(8,128)(2,1)S(1)} %get-tuple-element.64.a, bf16[192,1024]{1,0:T(8,128)(2,1)S(1)} %collective-permute-done.b, bf16[1024,1920]{1,0:T(8,128)(2,1)S(1)} %get-tuple-element.65.refs_0_, ...), custom_call_target="tpu_custom_call" | custom-call | flops 3019898880 | bytes 19464192 | tf_op jit(solution)/shard_map/project/pallas_call | solution.py:133
  71.7 11.7 %collective-permute-done.63.refs_4_ = bf16[2,32,1920]{2,1,0:T(8,128)(2,1)S(1)} collective-permute-done((bf16[2,32,1920]{2,1,0:T(8,128)(2,1)S(1)}, bf16[2,32,1920]{2,1,0:T(8,128)(2,1)S(1)}, u32[]{:S(2)}, u32[]{:S(2)}) %collective-permute-start.63) | collective-permute-done | bytes 245792 | tf_op jit(solution)/shard_map/ppermute | solution.py:262
  85.5 6.0 %project.14 = (f32[2,64,1920]{2,1,0:T(8,128)S(1)}, f32[2,64,1920]{2,1,0:T(8,128)S(1)}, f32[2,64,1920]{2,1,0:T(8,128)S(1)}, f32[2,64,1920]{2,1,0:T(8,128)S(1)}) custom-call(bf16[256,1024]{1,0:T(8,128)(2,1)S(1)} %get-tuple-element.83.a, bf16[256,1024]{1,0:T(8,128)(2,1)S(1)} %collective-permute-done.24.b, bf16[1024,1920]{1,0:T(8,128)(2,1)S(1)} %get-tuple-element.65.refs_0_, ...), custom_call_target="tpu_custom_call" | custom-call | flops 4026531840 | bytes 20709376 | tf_op jit(solution)/shard_map/project/pallas_call | solution.py:133
  93.8 4.8 %project.16 = (f32[2,48,1920]{2,1,0:T(8,128)S(1)}, f32[2,48,1920]{2,1,0:T(8,128)S(1)}, f32[2,48,1920]{2,1,0:T(8,128)S(1)}, f32[2,48,1920]{2,1,0:T(8,128)S(1)}) custom-call(bf16[192,1024]{1,0:T(8,128)(2,1)S(1)} %get-tuple-element.95.a, bf16[192,1024]{1,0:T(8,128)(2,1)S(1)} %collective-permute-done.41.b, bf16[1024,1920]{1,0:T(8,128)(2,1)S(1)} %get-tuple-element.65.refs_0_, ...), custom_call_target="tpu_custom_call" | custom-call | flops 3019898880 | bytes 19464192 | tf_op jit(solution)/shard_map/project/pallas_call | solution.py:133
  100.4 11.2 %collective-permute-done.12.refs_9_ = bf16[2,48,1920]{2,1,0:T(8,128)(2,1)S(1)} collective-permute-done((bf16[2,48,1920]{2,1,0:T(8,128)(2,1)S(1)}, bf16[2,48,1920]{2,1,0:T(8,128)(2,1)S(1)}, u32[]{:S(2)}, u32[]{:S(2)}) %collective-permute-start.12) | collective-permute-done | bytes 368672 | tf_op jit(solution)/shard_map/ppermute | solution.py:262
  112.0 7.6 %collective-permute-done.66.refs_2_ = bf16[2,32,1920]{2,1,0:T(8,128)(2,1)S(1)} collective-permute-done((bf16[2,32,1920]{2,1,0:T(8,128)(2,1)S(1)}, bf16[2,32,1920]{2,1,0:T(8,128)(2,1)S(1)}, u32[]{:S(2)}, u32[]{:S(2)}) %collective-permute-start.66) | collective-permute-done | bytes 245792 | tf_op jit(solution)/shard_map/ppermute | solution.py:262
  125.5 5.5 %collective-permute-done.45.refs_4_ = bf16[2,48,1920]{2,1,0:T(8,128)(2,1)S(1)} collective-permute-done((bf16[2,48,1920]{2,1,0:T(8,128)(2,1)S(1)}, bf16[2,48,1920]{2,1,0:T(8,128)(2,1)S(1)}, u32[]{:S(2)}, u32[]{:S(2)}) %collective-permute-start.45) | collective-permute-done | bytes 368672 | tf_op jit(solution)/shard_map/ppermute | solution.py:262
  132.7 5.2 %collective-permute-done.14.refs_2_ = bf16[2,48,1920]{2,1,0:T(8,128)(2,1)S(1)} collective-permute-done((bf16[2,48,1920]{2,1,0:T(8,128)(2,1)S(1)}, bf16[2,48,1920]{2,1,0:T(8,128)(2,1)S(1)}, u32[]{:S(2)}, u32[]{:S(2)}) %collective-permute-start.14) | collective-permute-done | bytes 368672 | tf_op jit(solution)/shard_map/ppermute | solution.py:262
  149.1 5.8 %collective-permute-done.28.refs_4_ = bf16[2,64,1920]{2,1,0:T(8,128)(2,1)S(1)} collective-permute-done((bf16[2,64,1920]{2,1,0:T(8,128)(2,1)S(1)}, bf16[2,64,1920]{2,1,0:T(8,128)(2,1)S(1)}, u32[]{:S(2)}, u32[]{:S(2)}) %collective-permute-start.28) | collective-permute-done | bytes 491552 | tf_op jit(solution)/shard_map/ppermute | solution.py:262
  157.4 5.2 %collective-permute-done.48.refs_2_ = bf16[2,48,1920]{2,1,0:T(8,128)(2,1)S(1)} collective-permute-done((bf16[2,48,1920]{2,1,0:T(8,128)(2,1)S(1)}, bf16[2,48,1920]{2,1,0:T(8,128)(2,1)S(1)}, u32[]{:S(2)}, u32[]{:S(2)}) %collective-permute-start.48) | collective-permute-done | bytes 368672 | tf_op jit(solution)/shard_map/ppermute | solution.py:262
  163.1 3.8 %collective-permute-start.76 = (bf16[2,32,1024]{2,1,0:T(8,128)(2,1)S(1)}, bf16[2,32,1024]{2,1,0:T(8,128)(2,1)S(1)}, u32[]{:S(2)}, u32[]{:S(2)}) collective-permute-start(bf16[2,32,1024]{2,1,0:T(8,128)(2,1)S(1)} %get-tuple-element.122), channel_id=1, source_target_pairs={{0,3},{1,2},{2,1},{3,0},{4,7},{5,6},{6,5},{7,4},{8,11},{9,10},{10,... | collective-permute-start | bytes 393224 | tf_op jit(solution)/shard_map/ppermute | solution.py:262
  192.2 4.7 %down.4 = (bf16[2,2,48,1024]{3,2,1,0:T(8,128)(2,1)S(1)}, f32[2,2,48,1024]{3,2,1,0:T(8,128)S(1)}) custom-call(s32[3]{0:T(128)S(1)} %pad_add_fusion.where_ref, bf16[2,48,1920]{2,1,0:T(8,128)(2,1)S(1)} %add_received.9.refs_0_, bf16[2,48,1920]{2,1,0:T(8,128)(2,1)S(1)} %collective-permute-done.13.refs_1_, ...), custom_call_target="tpu_custom_call" | custom-call | flops 3019898880 | bytes 11993088 | tf_op jit(solution)/shard_map/down/pallas_call | solution.py:239
  199.8 6.0 %down.5 = (bf16[2,2,64,1024]{3,2,1,0:T(8,128)(2,1)S(1)}, f32[2,2,64,1024]{3,2,1,0:T(8,128)S(1)}) custom-call(s32[3]{0:T(128)S(1)} %pad_add_fusion.where_ref, bf16[2,64,1920]{2,1,0:T(8,128)(2,1)S(1)} %add_received.11.refs_0_, bf16[2,64,1920]{2,1,0:T(8,128)(2,1)S(1)} %collective-permute-done.30.refs_1_, ...), custom_call_target="tpu_custom_call" | custom-call | flops 4026531840 | bytes 13369344 | tf_op jit(solution)/shard_map/down/pallas_call | solution.py:239
  206.2 4.7 %down.6 = (bf16[2,48,1024]{2,1,0:T(8,128)(2,1)S(1)}, bf16[2,48,1024]{2,1,0:T(8,128)(2,1)S(1)}, bf16[2,48,1024]{2,1,0:T(8,128)(2,1)S(1)}, f32[2,48,1024]{2,1,0:T(8,128)S(1)}) custom-call(s32[3]{0:T(128)S(1)} %pad_add_fusion.where_ref, bf16[2,48,1920]{2,1,0:T(8,128)(2,1)S(1)} %add_received.13.refs_0_, ...), custom_call_target="tpu_custom_call" | custom-call | flops 3019898880 | bytes 11993088 | tf_op jit(solution)/shard_map/down/pallas_call | solution.py:239
  210.9 3.9 %collective-permute-start.58 = (bf16[2,48,1024]{2,1,0:T(8,128)(2,1)S(1)}, bf16[2,48,1024]{2,1,0:T(8,128)(2,1)S(1)}, u32[]{:S(2)}, u32[]{:S(2)}) collective-permute-start(bf16[2,48,1024]{2,1,0:T(8,128)(2,1)S(1)} %get-tuple-element.108), channel_id=1, source_target_pairs={{0,3},{1,2},{2,1},{3,0},{4,7},{5,6},{6,5},{7,4},{8,11},{9,10},{10,... | collective-permute-start | bytes 589832 | tf_op jit(solution)/shard_map/ppermute | solution.py:262
  217.9 10.3 %collective-permute-done.39 = bf16[2,2,64,1024]{3,2,1,0:T(8,128)(2,1)S(1)} collective-permute-done((bf16[2,2,64,1024]{3,2,1,0:T(8,128)(2,1)S(1)}, bf16[2,2,64,1024]{3,2,1,0:T(8,128)(2,1)S(1)}, u32[]{:S(2)}, u32[]{:S(2)}) %collective-permute-start.39) | collective-permute-done | bytes 524320 | tf_op jit(solution)/shard_map/ppermute | solution.py:262
  228.4 4.1 %collective-permute-done.57 = bf16[2,48,1024]{2,1,0:T(8,128)(2,1)S(1)} collective-permute-done((bf16[2,48,1024]{2,1,0:T(8,128)(2,1)S(1)}, bf16[2,48,1024]{2,1,0:T(8,128)(2,1)S(1)}, u32[]{:S(2)}, u32[]{:S(2)}) %collective-permute-start.57) | collective-permute-done | bytes 196640 | tf_op jit(solution)/shard_map/ppermute | solution.py:262
  235.8 10.6 %collective-permute-done.23 = bf16[2,48,1024]{2,1,0:T(8,128)(2,1)S(1)} collective-permute-done((bf16[2,48,1024]{2,1,0:T(8,128)(2,1)S(1)}, bf16[2,48,1024]{2,1,0:T(8,128)(2,1)S(1)}, u32[]{:S(2)}, u32[]{:S(2)}) %collective-permute-start.23) | collective-permute-done | bytes 196640 | tf_op jit(solution)/shard_map/ppermute | solution.py:262
  246.5 4.6 %collective-permute-done.40 = bf16[2,64,1024]{2,1,0:T(8,128)(2,1)S(1)} collective-permute-done((bf16[2,64,1024]{2,1,0:T(8,128)(2,1)S(1)}, bf16[2,64,1024]{2,1,0:T(8,128)(2,1)S(1)}, u32[]{:S(2)}, u32[]{:S(2)}) %collective-permute-start.40) | collective-permute-done | bytes 262176 | tf_op jit(solution)/shard_map/ppermute | solution.py:262
  (188 shorter events, 105.7 us)
Async XLA Ops:
  28.7 21.2 %collective-permute-start.6 = (bf16[1,96,1280]{2,1,0:T(8,128)(2,1)S(1)}, bf16[1,96,1280]{2,1,0:T(8,128)(2,1)S(1)}, u32[]{:S(2)}, u32[]{:S(2)}) collective-permute-start(bf16[1,96,1280]{2,1,0:T(8,128)(2,1)S(1)} %get-tuple-element.72), channel_id=1, source_target_pairs={{0,8},{4,12},{8,0},{12,4},{16,24},{20,28},{24,16},{28,20},{1,9},{5... | collective-permute-start | bytes 737288 | tf_op jit(solution)/shard_map/ppermute | solution.py:262
  28.8 22.8 %collective-permute-start.9 = (bf16[1,96,1280]{2,1,0:T(8,128)(2,1)S(1)}, bf16[1,96,1280]{2,1,0:T(8,128)(2,1)S(1)}, u32[]{:S(2)}, u32[]{:S(2)}) collective-permute-start(bf16[1,96,1280]{2,1,0:T(8,128)(2,1)S(1)} %get-tuple-element.75), channel_id=1, source_target_pairs={{0,16},{4,20},{8,24},{12,28},{16,0},{20,4},{24,8},{28,12},{1,17},{... | collective-permute-start | bytes 737288 | tf_op jit(solution)/shard_map/ppermute | solution.py:262
  30.8 27.2 %collective-permute-start.61 = (bf16[2,64,1920]{2,1,0:T(8,128)(2,1)S(1)}, bf16[2,64,1920]{2,1,0:T(8,128)(2,1)S(1)}, u32[]{:S(2)}, u32[]{:S(2)}) collective-permute-start(bf16[2,64,1920]{2,1,0:T(8,128)(2,1)S(1)} %get-tuple-element.113), channel_id=1, source_target_pairs={{0,8},{4,12},{8,0},{12,4},{16,24},{20,28},{24,16},{28,20},{1,9},{5... | collective-permute-start | bytes 1474568 | tf_op jit(solution)/shard_map/ppermute | solution.py:262
  32.3 26.3 %collective-permute-start.62 = (bf16[2,64,1920]{2,1,0:T(8,128)(2,1)S(1)}, bf16[2,64,1920]{2,1,0:T(8,128)(2,1)S(1)}, u32[]{:S(2)}, u32[]{:S(2)}) collective-permute-start(bf16[2,64,1920]{2,1,0:T(8,128)(2,1)S(1)} %get-tuple-element.114), channel_id=1, source_target_pairs={{0,16},{4,20},{8,24},{12,28},{16,0},{20,4},{24,8},{28,12},{1,17},{... | collective-permute-start | bytes 1474568 | tf_op jit(solution)/shard_map/ppermute | solution.py:262
  50.0 21.1 %collective-permute-start.24 = (bf16[256,1024]{1,0:T(8,128)(2,1)S(1)}, bf16[256,1024]{1,0:T(8,128)(2,1)S(1)}, u32[]{:S(2)}, u32[]{:S(2)}) collective-permute-start(bf16[256,1024]{1,0:T(8,128)(2,1)S(1)} %get-tuple-element.83.a), channel_id=1, source_target_pairs={{0,4},{4,0},{8,12},{12,8},{16,20},{20,16},{24,28},{28,24},{1,5},{5... | collective-permute-start | bytes 1572872 | tf_op jit(solution)/shard_map/ppermute | solution.py:262
  58.0 33.7 %collective-permute-start.43 = (bf16[2,96,1920]{2,1,0:T(8,128)(2,1)S(1)}, bf16[2,96,1920]{2,1,0:T(8,128)(2,1)S(1)}, u32[]{:S(2)}, u32[]{:S(2)}) collective-permute-start(bf16[2,96,1920]{2,1,0:T(8,128)(2,1)S(1)} %get-tuple-element.99), channel_id=1, source_target_pairs={{0,8},{4,12},{8,0},{12,4},{16,24},{20,28},{24,16},{28,20},{1,9},{5... | collective-permute-start | bytes 2211848 | tf_op jit(solution)/shard_map/ppermute | solution.py:262
  58.6 33.5 %collective-permute-start.44 = (bf16[2,96,1920]{2,1,0:T(8,128)(2,1)S(1)}, bf16[2,96,1920]{2,1,0:T(8,128)(2,1)S(1)}, u32[]{:S(2)}, u32[]{:S(2)}) collective-permute-start(bf16[2,96,1920]{2,1,0:T(8,128)(2,1)S(1)} %get-tuple-element.100), channel_id=1, source_target_pairs={{0,16},{4,20},{8,24},{12,28},{16,0},{20,4},{24,8},{28,12},{1,17},{... | collective-permute-start | bytes 2211848 | tf_op jit(solution)/shard_map/ppermute | solution.py:262
  62.6 20.8 %collective-permute-start.63 = (bf16[2,32,1920]{2,1,0:T(8,128)(2,1)S(1)}, bf16[2,32,1920]{2,1,0:T(8,128)(2,1)S(1)}, u32[]{:S(2)}, u32[]{:S(2)}) collective-permute-start(bf16[2,32,1920]{2,1,0:T(8,128)(2,1)S(1)} %get-tuple-element.117), channel_id=1, source_target_pairs={{0,16},{4,20},{8,24},{12,28},{16,0},{20,4},{24,8},{28,12},{1,17},{... | collective-permute-start | bytes 737288 | tf_op jit(solution)/shard_map/ppermute | solution.py:262
  64.4 20.5 %collective-permute-start.64 = (bf16[2,32,1920]{2,1,0:T(8,128)(2,1)S(1)}, bf16[2,32,1920]{2,1,0:T(8,128)(2,1)S(1)}, u32[]{:S(2)}, u32[]{:S(2)}) collective-permute-start(bf16[2,32,1920]{2,1,0:T(8,128)(2,1)S(1)} %get-tuple-element.118), channel_id=1, source_target_pairs={{0,8},{4,12},{8,0},{12,4},{16,24},{20,28},{24,16},{28,20},{1,9},{5... | collective-permute-start | bytes 737288 | tf_op jit(solution)/shard_map/ppermute | solution.py:262
  71.0 50.7 %collective-permute-start.26 = (bf16[2,128,1920]{2,1,0:T(8,128)(2,1)S(1)}, bf16[2,128,1920]{2,1,0:T(8,128)(2,1)S(1)}, u32[]{:S(2)}, u32[]{:S(2)}) collective-permute-start(bf16[2,128,1920]{2,1,0:T(8,128)(2,1)S(1)} %get-tuple-element.87), channel_id=1, source_target_pairs={{0,8},{4,12},{8,0},{12,4},{16,24},{20,28},{24,16},{28,20},{1,9},{5... | collective-permute-start | bytes 2949128 | tf_op jit(solution)/shard_map/ppermute | solution.py:262
  84.9 26.7 %collective-permute-start.12 = (bf16[2,48,1920]{2,1,0:T(8,128)(2,1)S(1)}, bf16[2,48,1920]{2,1,0:T(8,128)(2,1)S(1)}, u32[]{:S(2)}, u32[]{:S(2)}) collective-permute-start(bf16[2,48,1920]{2,1,0:T(8,128)(2,1)S(1)} %get-tuple-element.80), channel_id=1, source_target_pairs={{0,8},{4,12},{8,0},{12,4},{16,24},{20,28},{24,16},{28,20},{1,9},{5... | collective-permute-start | bytes 1105928 | tf_op jit(solution)/shard_map/ppermute | solution.py:262
  91.7 31.4 %collective-permute-start.27 = (bf16[2,128,1920]{2,1,0:T(8,128)(2,1)S(1)}, bf16[2,128,1920]{2,1,0:T(8,128)(2,1)S(1)}, u32[]{:S(2)}, u32[]{:S(2)}) collective-permute-start(bf16[2,128,1920]{2,1,0:T(8,128)(2,1)S(1)} %get-tuple-element.88), channel_id=1, source_target_pairs={{0,16},{4,20},{8,24},{12,28},{16,0},{20,4},{24,8},{28,12},{1,17},{... | collective-permute-start | bytes 2949128 | tf_op jit(solution)/shard_map/ppermute | solution.py:262
  92.1 27.5 %collective-permute-start.66 = (bf16[2,32,1920]{2,1,0:T(8,128)(2,1)S(1)}, bf16[2,32,1920]{2,1,0:T(8,128)(2,1)S(1)}, u32[]{:S(2)}, u32[]{:S(2)}) collective-permute-start(bf16[2,32,1920]{2,1,0:T(8,128)(2,1)S(1)} %add_received.15.refs_0_), channel_id=1, source_target_pairs={{0,16},{4,20},{8,24},{12,28},{16,0},{20,4},{24,8},{28,12},{1,17},{... | collective-permute-start | bytes 737288 | tf_op jit(solution)/shard_map/ppermute | solution.py:262
  98.8 22.3 %collective-permute-start.65 = (bf16[2,32,1920]{2,1,0:T(8,128)(2,1)S(1)}, bf16[2,32,1920]{2,1,0:T(8,128)(2,1)S(1)}, u32[]{:S(2)}, u32[]{:S(2)}) collective-permute-start(bf16[2,32,1920]{2,1,0:T(8,128)(2,1)S(1)} %add_received.15.refs_0_), channel_id=1, source_target_pairs={{0,8},{4,12},{8,0},{12,4},{16,24},{20,28},{24,16},{28,20},{1,9},{5... | collective-permute-start | bytes 737288 | tf_op jit(solution)/shard_map/ppermute | solution.py:262
  123.1 18.7 %collective-permute-start.13 = (bf16[2,48,1920]{2,1,0:T(8,128)(2,1)S(1)}, bf16[2,48,1920]{2,1,0:T(8,128)(2,1)S(1)}, u32[]{:S(2)}, u32[]{:S(2)}) collective-permute-start(bf16[2,48,1920]{2,1,0:T(8,128)(2,1)S(1)} %add_received.9.refs_0_), channel_id=1, source_target_pairs={{0,8},{4,12},{8,0},{12,4},{16,24},{20,28},{24,16},{28,20},{1,9},{5... | collective-permute-start | bytes 1105928 | tf_op jit(solution)/shard_map/ppermute | solution.py:262
  142.3 20.2 %collective-permute-start.48 = (bf16[2,48,1920]{2,1,0:T(8,128)(2,1)S(1)}, bf16[2,48,1920]{2,1,0:T(8,128)(2,1)S(1)}, u32[]{:S(2)}, u32[]{:S(2)}) collective-permute-start(bf16[2,48,1920]{2,1,0:T(8,128)(2,1)S(1)} %add_received.13.refs_0_), channel_id=1, source_target_pairs={{0,16},{4,20},{8,24},{12,28},{16,0},{20,4},{24,8},{28,12},{1,17},{... | collective-permute-start | bytes 1105928 | tf_op jit(solution)/shard_map/ppermute | solution.py:262
  143.6 19.4 %collective-permute-start.17 = (bf16[2,48,1920]{2,1,0:T(8,128)(2,1)S(1)}, bf16[2,48,1920]{2,1,0:T(8,128)(2,1)S(1)}, u32[]{:S(2)}, u32[]{:S(2)}) collective-permute-start(bf16[2,48,1920]{2,1,0:T(8,128)(2,1)S(1)} %add_received.9.refs_0_), channel_id=1, source_target_pairs={{0,4},{4,0},{8,12},{12,8},{16,20},{20,16},{24,28},{28,24},{1,5},{5... | collective-permute-start | bytes 1105928 | tf_op jit(solution)/shard_map/ppermute | solution.py:262
  143.7 23.2 %collective-permute-start.47 = (bf16[2,48,1920]{2,1,0:T(8,128)(2,1)S(1)}, bf16[2,48,1920]{2,1,0:T(8,128)(2,1)S(1)}, u32[]{:S(2)}, u32[]{:S(2)}) collective-permute-start(bf16[2,48,1920]{2,1,0:T(8,128)(2,1)S(1)} %add_received.13.refs_0_), channel_id=1, source_target_pairs={{0,8},{4,12},{8,0},{12,4},{16,24},{20,28},{24,16},{28,20},{1,9},{5... | collective-permute-start | bytes 1105928 | tf_op jit(solution)/shard_map/ppermute | solution.py:262
  196.9 18.5 %collective-permute-start.22 = (bf16[2,2,48,1024]{3,2,1,0:T(8,128)(2,1)S(1)}, bf16[2,2,48,1024]{3,2,1,0:T(8,128)(2,1)S(1)}, u32[]{:S(2)}, u32[]{:S(2)}) collective-permute-start(bf16[2,2,48,1024]{3,2,1,0:T(8,128)(2,1)S(1)} %get-tuple-element.82), channel_id=1, source_target_pairs={{0,1},{1,0},{2,3},{3,2},{4,5},{5,4},{6,7},{7,6},{8,9},{9,8},{10,11... | collective-permute-start | bytes 1179656 | tf_op jit(solution)/shard_map/ppermute | solution.py:262
  205.9 22.3 %collective-permute-start.39 = (bf16[2,2,64,1024]{3,2,1,0:T(8,128)(2,1)S(1)}, bf16[2,2,64,1024]{3,2,1,0:T(8,128)(2,1)S(1)}, u32[]{:S(2)}, u32[]{:S(2)}) collective-permute-start(bf16[2,2,64,1024]{3,2,1,0:T(8,128)(2,1)S(1)} %get-tuple-element.94), channel_id=1, source_target_pairs={{0,1},{1,0},{2,3},{3,2},{4,5},{5,4},{6,7},{7,6},{8,9},{9,8},{10,11... | collective-permute-start | bytes 1572872 | tf_op jit(solution)/shard_map/ppermute | solution.py:262
  214.8 17.6 %collective-permute-start.57 = (bf16[2,48,1024]{2,1,0:T(8,128)(2,1)S(1)}, bf16[2,48,1024]{2,1,0:T(8,128)(2,1)S(1)}, u32[]{:S(2)}, u32[]{:S(2)}) collective-permute-start(bf16[2,48,1024]{2,1,0:T(8,128)(2,1)S(1)} %get-tuple-element.107), channel_id=1, source_target_pairs={{0,2},{1,3},{2,0},{3,1},{4,6},{5,7},{6,4},{7,5},{8,10},{9,11},{10,... | collective-permute-start | bytes 589832 | tf_op jit(solution)/shard_map/ppermute | solution.py:262
  214.8 20.9 %collective-permute-start.56 = (bf16[2,48,1024]{2,1,0:T(8,128)(2,1)S(1)}, bf16[2,48,1024]{2,1,0:T(8,128)(2,1)S(1)}, u32[]{:S(2)}, u32[]{:S(2)}) collective-permute-start(bf16[2,48,1024]{2,1,0:T(8,128)(2,1)S(1)} %get-tuple-element.106), channel_id=1, source_target_pairs={{0,1},{1,0},{2,3},{3,2},{4,5},{5,4},{6,7},{7,6},{8,9},{9,8},{10,11... | collective-permute-start | bytes 589832 | tf_op jit(solution)/shard_map/ppermute | solution.py:262
  215.5 30.9 %collective-permute-start.23 = (bf16[2,48,1024]{2,1,0:T(8,128)(2,1)S(1)}, bf16[2,48,1024]{2,1,0:T(8,128)(2,1)S(1)}, u32[]{:S(2)}, u32[]{:S(2)}) collective-permute-start(bf16[2,48,1024]{2,1,0:T(8,128)(2,1)S(1)} %fusion.3), channel_id=1, source_target_pairs={{0,2},{1,3},{2,0},{3,1},{4,6},{5,7},{6,4},{7,5},{8,10},{9,11},{10,... | collective-permute-start | bytes 589832 | tf_op jit(solution)/shard_map/ppermute | solution.py:262
  228.2 22.9 %collective-permute-start.40 = (bf16[2,64,1024]{2,1,0:T(8,128)(2,1)S(1)}, bf16[2,64,1024]{2,1,0:T(8,128)(2,1)S(1)}, u32[]{:S(2)}, u32[]{:S(2)}) collective-permute-start(bf16[2,64,1024]{2,1,0:T(8,128)(2,1)S(1)} %fusion.2), channel_id=1, source_target_pairs={{0,2},{1,3},{2,0},{3,1},{4,6},{5,7},{6,4},{7,5},{8,10},{9,11},{10,... | collective-permute-start | bytes 786440 | tf_op jit(solution)/shard_map/ppermute | solution.py:262
  (58 other events, 602.6 us)
